TPU v7x, 128 devices: a whole 4x4x4 slice. The times are simulated.
128 devices in a mesh: frame: 8 (over x_hi, z), pos: 16 (over y, x_lo, core).
Axes of the slice: x: 4 (x_hi: 2, x_lo: 2; x = x_hi * 2 + x_lo), y: 4, z: 4, core: 2. Of those that a mesh axis runs over, the one named last changes fastest.
Arguments:
- latents: bfloat16 [256, 1024, 256], P('frame', 'pos'), as said below
- gain_one: float32 [256], replicated, may hold values from 0.5 to 1.5
- query_one: bfloat16 [256, 256], replicated, as said below
- key_one: bfloat16 [256, 256], replicated, as said below
- value_one: bfloat16 [256, 256], replicated, may hold values from -0.375 to 0.375
- out_one: bfloat16 [256, 256], replicated, may hold values from -0.75 to 0.75
- gain_two: float32 [256], replicated, may hold values from 0.5 to 1.5
- query_two: bfloat16 [256, 256], replicated, as said below
- key_two: bfloat16 [256, 256], replicated, as said below
- value_two: bfloat16 [256, 256], replicated, may hold values from -0.375 to 0.375
- out_two: bfloat16 [256, 256], replicated, may hold values from -0.75 to 0.75
Outputs:
- decoded: bfloat16 [256, 1024, 256], P('frame', 'pos')
Inputs may be any that keep to these rules, and one draw needn't show every extreme that they name: `latents`: latent features of the video. `query_one`: A projection of the spatial block. `key_one`: A projection of the spatial block. `query_two`: A projection of the temporal block. `key_two`: A projection of the temporal block.
All inputs are finite; a program needn't handle non-finite values.
Results may differ from a plain program's by a relative error of at most 0.015.
The roundings to bfloat16 on the way count: a program that leaves them out, or rounds other values in their place, can miss the bound.
Values may be sent and summed in bfloat16 or wider, within the bound.
A program may use at most 320 MiB of HBM per device.

v0:
```python
import jax
import jax.numpy as jnp
from jax import lax
from jax.sharding import PartitionSpec as P

HEADS = 4


def normed(values, gain):
    wide = values.astype(jnp.float32)
    factor = lax.rsqrt(jnp.mean(wide * wide, axis=-1, keepdims=True) + 1e-06)
    return (wide * factor * gain).astype(jnp.bfloat16)


def project(values, weight):
    flat = values.reshape(-1, values.shape[-1])
    result = jnp.dot(flat, weight, preferred_element_type=jnp.float32).astype(jnp.bfloat16)
    return result.reshape(values.shape[:-1] + (weight.shape[1],))


def heads_of(values):
    return values.reshape(values.shape[:-1] + (HEADS, values.shape[-1] // HEADS))


def softmax_attend(query, keys, vals, score_form, value_form, total_form):
    scale = query.shape[-1] ** (-0.5)
    scores = jnp.einsum(score_form, query, keys, preferred_element_type=jnp.float32) * scale
    weights = jnp.exp(scores - jnp.max(scores, axis=-1, keepdims=True))
    totals = jnp.sum(weights, axis=-1)
    summed = jnp.einsum(
        value_form, weights.astype(jnp.bfloat16), vals, preferred_element_type=jnp.float32
    )
    return summed / jnp.einsum(total_form, totals)[..., None]


def shards(
    latents,
    gain_one,
    query_one,
    key_one,
    value_one,
    out_one,
    gain_two,
    query_two,
    key_two,
    value_two,
    out_two,
):
    frames, places, width = latents.shape
    n_pos = lax.axis_size("pos")
    n_frame = lax.axis_size("frame")
    per = frames // n_pos
    first = jnp.where(lax.axis_index("frame") == 0, latents[0], 0).astype(latents.dtype)
    first = lax.psum(first, "frame")
    sent = jnp.concatenate(
        [
            latents.reshape(n_pos, per, places, width),
            jnp.broadcast_to(first[None, None], (n_pos, 1, places, width)),
        ],
        axis=1,
    )
    got = lax.all_to_all(sent, "pos", 0, 0, tiled=True)
    xs = got[:, :per].transpose(1, 0, 2, 3).reshape(per, n_pos * places, width)
    x0 = got[:, per].reshape(n_pos * places, width)
    n_one = normed(xs, gain_one)
    q_one = heads_of(project(n_one, query_one))
    k_one = heads_of(project(n_one, key_one))
    v_one = heads_of(project(n_one, value_one))
    n_zero = normed(x0, gain_one)
    k_zero = heads_of(project(n_zero, key_one))
    v_zero = heads_of(project(n_zero, value_one))
    keys = jnp.concatenate([k_one, jnp.broadcast_to(k_zero[None], k_one.shape)], axis=1)
    vals = jnp.concatenate([v_one, jnp.broadcast_to(v_zero[None], v_one.shape)], axis=1)
    attended_one = (
        softmax_attend(q_one, keys, vals, "fphd,fkhd->fhpk", "fhpk,fkhd->fphd", "fhp->fph")
        .reshape(xs.shape)
        .astype(jnp.bfloat16)
    )
    mixed_one = jnp.dot(
        attended_one.reshape(-1, width), out_one, preferred_element_type=jnp.float32
    ).reshape(xs.shape)
    middle = (xs.astype(jnp.float32) + mixed_one).astype(jnp.bfloat16)
    all_places = n_pos * places
    run = all_places // (n_pos * n_frame)
    sent = (
        middle.reshape(per, n_pos, n_frame, run, width)
        .transpose(2, 1, 0, 3, 4)
        .reshape(n_frame * n_pos, per, run, width)
    )
    got = lax.all_to_all(sent, ("frame", "pos"), 0, 0, tiled=True)
    mid_t = got.reshape(n_frame * n_pos * per, run, width)
    n_two = normed(mid_t, gain_two)
    q_two = heads_of(project(n_two, query_two))
    k_two = heads_of(project(n_two, key_two))
    v_two = heads_of(project(n_two, value_two))
    attended_two = (
        softmax_attend(q_two, k_two, v_two, "fphd,kphd->phfk", "phfk,kphd->fphd", "phf->fph")
        .reshape(mid_t.shape)
        .astype(jnp.bfloat16)
    )
    mixed_two = jnp.dot(
        attended_two.reshape(-1, width), out_two, preferred_element_type=jnp.float32
    ).reshape(mid_t.shape)
    decoded = (mid_t.astype(jnp.float32) + mixed_two).astype(jnp.bfloat16)
    sent = decoded.reshape(n_frame, frames, run, width)
    got = lax.all_to_all(sent, "frame", 0, 0, tiled=True)
    return got.transpose(1, 0, 2, 3).reshape(frames, places, width)


def solution(mesh):
    return jax.shard_map(
        shards,
        mesh=mesh,
        in_specs=(P("frame", "pos", None), P(), P(), P(), P(), P(), P(), P(), P(), P(), P()),
        out_specs=P("frame", "pos", None),
        check_vma=False,
    )
```

profile of v0, /device:TPU:0, one launch (start us, length us, event | category | flops | bytes accessed | tf_op | source)
XLA Modules:
  0.0 243.1 jit_solution(5843305531094082782)
XLA Ops:
  0.0 0.8 select_bitcast_fusion
  0.8 43.1 %psum.7 = bf16[64,256]{1,0:T(8,128)(2,1)S(1)} all-reduce(bf16[64,256]{1,0:T(8,128)(2,1)S(1)} %select_bitcast_fusion), channel_id=1, replica_groups=mesh['frame'=8,'pos'=16] {'frame'}, use_global_device_ids=true, to_apply=%region_0.1 | all-reduce | flops 16384 | bytes 65536 | tf_op jit(solution)/shard_map/psum | solution.py:54
  44.0 1.4 pad_maximum_fusion
  45.3 26.5 %all_to_all.15 = bf16[16,3,64,256]{3,2,1,0:T(8,128)(2,1)S(1)} all-to-all(bf16[16,3,64,256]{3,2,1,0:T(8,128)(2,1)S(1)} %pad_maximum_fusion), channel_id=1, replica_groups=mesh['frame'=8,'pos'=16] {'pos'}, dimensions={0} | all-to-all | bytes 3145728 | tf_op jit(solution)/shard_map/all_to_all | solution.py:62
  71.9 0.3 multiply_reduce_fusion.3
  72.3 0.2 multiply_reduce_fusion.4
  72.5 0.5 copy-done.1
  73.1 1.5 copy_convert_fusion
  74.6 0.3 fusion.18
  74.9 1.4 convolution_convert_fusion.3
  76.3 1.2 slice_convert_fusion
  77.5 0.2 fusion.35
  77.7 1.1 convolution_convert_fusion.6
  78.9 1.4 convolution_convert_fusion.5
  80.3 1.1 convolution_convert_fusion.7
  81.4 4.5 %reshape.135 = bf16[2,1024,4,64]{3,2,1,0:T(4,128)(2,1)} reshape(bf16[2048,256]{1,0:T(8,128)(2,1)} %convolution_convert_fusion.3) | data formatting | bytes 2097152 | tf_op jit(solution)/shard_map/reshape;reshape | solution.py:22
  85.9 4.1 %copy.61 = bf16[2,1024,4,64]{1,3,2,0:T(8,128)(2,1)} copy(bf16[2,1024,4,64]{3,2,1,0:T(4,128)(2,1)} %reshape.135) | data formatting | bytes 2097152 | tf_op jit(solution)/shard_map/reshape;reshape | solution.py:22
  89.9 1.4 convolution_convert_fusion.4
  91.4 4.5 %reshape.134 = bf16[2,1024,4,64]{3,2,1,0:T(4,128)(2,1)} reshape(bf16[2048,256]{1,0:T(8,128)(2,1)} %convolution_convert_fusion.4) | data formatting | bytes 2097152 | tf_op jit(solution)/shard_map/reshape;reshape | solution.py:22
  95.9 1.9 reshape.133
  97.8 4.2 %copy.58 = bf16[2,1024,4,64]{1,3,2,0:T(8,128)(2,1)} copy(bf16[2,1024,4,64]{3,2,1,0:T(4,128)(2,1)} %reshape.133) | data formatting | bytes 2097152 | tf_op jit(solution)/shard_map/reshape;reshape | solution.py:22
  101.9 1.2 broadcast_in_dim.19
  103.1 24.7 %multiply_reduce_fusion = (f32[2,4,1024]{2,1,0:T(4,128)S(1)}, f32[2,4,1024,2048]{3,2,1,0:T(8,128)}) fusion(bf16[2,1024,4,64]{1,3,2,0:T(8,128)(2,1)S(1)} %broadcast_in_dim.19, bf16[2,1024,4,64]{1,3,2,0:T(8,128)(2,1)S(1)} %copy-done.3, bf16[2,1024,4,64]{3,2,1,0:T(4,128)(2,1)} %reshape.134), kind=kOutput, calls=%fused_computation.1 | convolution fusion | flops 2185224192 | bytes 70287360 | tf_op jit(solution)/shard_map/fphd,fkhd->fhpk/dot_general | solution.py:27
  127.8 21.2 %fusion = f32[2,4,1024]{2,1,0:T(4,128)S(1)} fusion(f32[2,4,1024,2048]{3,2,1,0:T(8,128)} %get-tuple-element.6, f32[2,4,1024]{2,1,0:T(4,128)S(1)} %get-tuple-element.5), kind=kLoop, calls=%fused_computation.2 | loop fusion | flops 50323456 | bytes 67174400 | tf_op jit(solution)/shard_map/reduce_sum | solution.py:29
  149.1 2.2 broadcast_in_dim.17
  151.3 24.9 %fusion.24 = bf16[2,1024,4,64]{1,3,2,0:T(8,128)(2,1)} fusion(f32[2,4,1024,2048]{3,2,1,0:T(8,128)} %get-tuple-element.6, f32[2,4,1024]{2,1,0:T(4,128)S(1)} %get-tuple-element.5, bf16[2,1024,4,64]{1,3,2,0:T(8,128)(2,1)} %broadcast_in_dim.17, bf16[2,1024,4,64]{1,3,2,0:T(8,128)(2,1)S(1)} %copy-done.4, f32[2,1024,4]{1,2,0:T(4,128)S(1)} %bitcast.88), kind=kOutput, calls=%fused_computation.38 | convolution fusion | flops 2203058176 | bytes 70320128 | tf_op jit(solution)/shard_map/fhpk,fkhd->fphd/dot_general | solution.py:30
  176.3 1.7 fusion.19
  178.0 0.1 copy.64
  178.1 23.2 %all_to_all.16 = bf16[128,2,8,256]{3,2,1,0:T(8,128)(2,1)S(1)} all-to-all(bf16[128,2,8,256]{3,2,1,0:T(8,128)(2,1)S(1)} %bitcast.80), channel_id=1, replica_groups=mesh['frame'=8,'pos'=16] {'frame','pos'}, dimensions={0} | all-to-all | bytes 2097152 | tf_op jit(solution)/shard_map/all_to_all | solution.py:90
  201.3 0.5 multiply_reduce_fusion.2
  201.7 0.1 add_rsqrt_fusion
  201.8 0.2 rsqrt.38
  202.0 0.3 fusion.22
  202.4 0.4 convolution_convert_fusion.1
  202.8 1.8 reshape_reshape.22
  204.7 0.4 convolution_convert_fusion
  205.1 1.9 reshape_reshape.23
  207.0 1.4 convolution_convert_fusion.2
  208.4 4.6 %reshape_reshape.21 = bf16[256,8,4,64]{3,2,1,0:T(4,128)(2,1)} reshape(bf16[2048,256]{1,0:T(8,128)(2,1)} %convolution_convert_fusion.2) | data formatting | bytes 2097152 | tf_op jit(solution)/shard_map/reshape;reshape | solution.py:22
  213.0 3.6 %multiply_reduce_fusion.1 = (f32[8,4,256]{2,1,0:T(4,128)S(1)}, f32[8,4,256,256]{2,3,1,0:T(8,128)S(1)}) fusion(bf16[256,8,4,64]{3,2,1,0:T(4,128)(2,1)} %reshape_reshape.23, bf16[256,8,4,64]{3,2,1,0:T(4,128)(2,1)S(1)} %copy-done.2), kind=kOutput, calls=%fused_computation.6 | convolution fusion | flops 272621568 | bytes 10518528 | tf_op jit(solution)/shard_map/fphd,kphd->phfk/dot_general | solution.py:27
  216.6 1.5 fusion.4
  218.2 1.9 fusion.20
  220.1 0.2 bitcast_convert_fusion
  220.3 0.7 copy-done.13
  221.0 0.9 fusion.23
  221.9 0.1 copy.71
  222.0 19.6 %all_to_all.17 = bf16[8,32,8,256]{3,1,2,0:T(8,128)(2,1)S(1)} all-to-all(bf16[8,32,8,256]{3,1,2,0:T(8,128)(2,1)S(1)} %copy.71), channel_id=1, replica_groups=mesh['frame'=8,'pos'=16] {'frame'}, dimensions={0} | all-to-all | bytes 2097152 | tf_op jit(solution)/shard_map/all_to_all | solution.py:106
  241.6 1.6 copy.72
  (35 shorter events, 0.3 us)
Async XLA Ops:
  0.0 74.9 %copy-start = (bf16[256,256]{1,0:T(8,128)(2,1)S(1)}, bf16[256,256]{1,0:T(8,128)(2,1)}, u32[]{:S(2)}) copy-start(bf16[256,256]{1,0:T(8,128)(2,1)} %param.14) | copy-start | bytes 393220
  71.9 1.2 copy-start.1
  72.2 2.3 copy-start.14
  76.3 2.5 %copy-start.7 = (bf16[256,256]{1,0:T(8,128)(2,1)S(1)}, bf16[256,256]{1,0:T(8,128)(2,1)}, u32[]{:S(2)}) copy-start(bf16[256,256]{1,0:T(8,128)(2,1)} %param.15) | copy-start | bytes 393220
  85.9 4.1 %copy-start.8 = (bf16[256,256]{1,0:T(8,128)(2,1)S(1)}, bf16[256,256]{1,0:T(8,128)(2,1)}, u32[]{:S(2)}) copy-start(bf16[256,256]{1,0:T(8,128)(2,1)} %param.13) | copy-start | bytes 393220
  91.4 4.5 %copy-start.5 = (bf16[2048,256]{1,0:T(8,128)(2,1)S(1)}, bf16[2048,256]{1,0:T(8,128)(2,1)}, u32[]{:S(2)}) copy-start(bf16[2048,256]{1,0:T(8,128)(2,1)} %convolution_convert_fusion.5) | copy-start | bytes 3145732
  97.8 5.3 %copy-start.3 = (bf16[2,1024,4,64]{1,3,2,0:T(8,128)(2,1)S(1)}, bf16[2,1024,4,64]{1,3,2,0:T(8,128)(2,1)}, u32[]{:S(2)}) copy-start(bf16[2,1024,4,64]{1,3,2,0:T(8,128)(2,1)} %copy.61) | copy-start | bytes 3145732
  149.1 2.2 copy-start.4
  151.3 24.9 %copy-start.9 = (bf16[256,256]{1,0:T(8,128)(2,1)S(1)}, bf16[256,256]{1,0:T(8,128)(2,1)}, u32[]{:S(2)}) copy-start(bf16[256,256]{1,0:T(8,128)(2,1)} %param.16) | copy-start | bytes 393220
  178.1 24.0 %copy-start.15 = (f32[256]{0:T(256)S(1)}, f32[256]{0:T(256)}, u32[]{:S(2)}) copy-start(f32[256]{0:T(256)} %param.17) | copy-start | bytes 3076
  201.3 1.1 copy-start.10
  202.8 1.8 copy-start.11
  205.1 1.9 copy-start.12
  208.4 4.6 %copy-start.2 = (bf16[256,8,4,64]{3,2,1,0:T(4,128)(2,1)S(1)}, bf16[256,8,4,64]{3,2,1,0:T(4,128)(2,1)}, u32[]{:S(2)}) copy-start(bf16[256,8,4,64]{3,2,1,0:T(4,128)(2,1)} %reshape_reshape.22) | copy-start | bytes 3145732
  216.6 1.6 copy-start.6
  220.1 0.9 copy-start.13
where the time goes:
time: 244 us; the launch traced here: 243 us
  blocking collectives  112 us (46%)
  matrix products  66.5 us (27%)
  local copies, waits for them, and re-layouts  34.1 us (14%)
  other arithmetic  29.8 us (12%)
    psum x1, blocking collectives, shards(): first = lax.psum(first, 'frame')  43.1 us
    dot_general x2, matrix products, softmax_attend(): jnp.einsum(score_form, query, keys, preferred_element_type=jnp.float32)  28.3 us
    another operation x8, local copies, waits for them, and re-layouts, heads_of(): values.reshape(values.shape[:-1] + (HEADS, values.shape[-1] // HEADS))  27.4 us
    dot_general x2, matrix products, softmax_attend(): jnp.einsum(value_form, weights.astype(jnp.bfloat16), vals, preferred_elem...  26.9 us
    all_to_all x1, blocking collectives, shards(): got = lax.all_to_all(sent, 'pos', 0, 0, tiled=True)  26.5 us
    all_to_all x1, blocking collectives, shards(): got = lax.all_to_all(sent, ('frame', 'pos'), 0, 0, tiled=True)  23.2 us
    reduce_sum x2, other arithmetic, softmax_attend(): totals = jnp.sum(weights, axis=-1)  22.8 us
    all_to_all x1, blocking collectives, shards(): got = lax.all_to_all(sent, 'frame', 0, 0, tiled=True)  19.6 us

commit v1 on v0

--- a/solution.py
+++ b/solution.py
@@ -1,9 +1,18 @@
+import functools
 import jax
 import jax.numpy as jnp
 from jax import lax
 from jax.sharding import PartitionSpec as P
 
 HEADS = 4
+
+
+def cover_views_by_axis(message, net_axis):
+    arr_now = jax.lax.all_gather(message, axis_name=net_axis)
+    return jnp.sum(arr_now, 0)
+
+
+place_groups_on_mesh = functools.partial(cover_views_by_axis, net_axis="frame")
 
 
 def normed(values, gain):
@@ -51,7 +60,7 @@
     n_frame = lax.axis_size("frame")
     per = frames // n_pos
     first = jnp.where(lax.axis_index("frame") == 0, latents[0], 0).astype(latents.dtype)
-    first = lax.psum(first, "frame")
+    first = place_groups_on_mesh(first)
     sent = jnp.concatenate(
         [
             latents.reshape(n_pos, per, places, width),

time: 244 us -> 241 us (0.988)
  blocking collectives: 112 us -> 109 us
    psum x1 -> x0, blocking collectives: 43.1 us -> none  [shards(): first = lax.psum(first, 'frame')]
    all_gather x0 -> x1, blocking collectives: none -> 35.7 us  [cover_views_by_axis(): arr_now = jax.lax.all_gather(message, axis_name=net_axis)]
    all_to_all x1, blocking collectives: 23.2 us -> 27.2 us  [shards(): got = lax.all_to_all(sent, ('frame', 'pos'), 0, 0, tiled=True)]
where the time goes in v1:
time: 241 us; the launch traced here: 240 us
  blocking collectives  109 us (45%)
  matrix products  66.5 us (28%)
  local copies, waits for them, and re-layouts  34.1 us (14%)
  other arithmetic  29.9 us (12%)
    all_gather x1, blocking collectives, cover_views_by_axis(): arr_now = jax.lax.all_gather(message, axis_name=net_axis)  35.7 us
    dot_general x2, matrix products, softmax_attend(): jnp.einsum(score_form, query, keys, preferred_element_type=jnp.float32)  28.3 us
    another operation x8, local copies, waits for them, and re-layouts, heads_of(): values.reshape(values.shape[:-1] + (HEADS, values.shape[-1] // HEADS))  27.4 us
    all_to_all x1, blocking collectives, shards(): got = lax.all_to_all(sent, ('frame', 'pos'), 0, 0, tiled=True)  27.2 us
    dot_general x2, matrix products, softmax_attend(): jnp.einsum(value_form, weights.astype(jnp.bfloat16), vals, preferred_elem...  26.9 us
    all_to_all x1, blocking collectives, shards(): got = lax.all_to_all(sent, 'pos', 0, 0, tiled=True)  26.5 us
    reduce_sum x2, other arithmetic, softmax_attend(): totals = jnp.sum(weights, axis=-1)  22.8 us
    all_to_all x1, blocking collectives, shards(): got = lax.all_to_all(sent, 'frame', 0, 0, tiled=True)  19.6 us

profile of v1, /device:TPU:0, one launch (start us, length us, event | category | flops | bytes accessed | tf_op | source)
XLA Modules:
  0.0 239.8 jit_solution(6449035921585722603)
XLA Ops:
  0.0 0.8 slice_select_fusion
  0.8 35.7 %all_gather.4 = bf16[8,64,256]{2,1,0:T(8,128)(2,1)S(1)} all-gather(bf16[1,64,256]{2,1,0:T(8,128)(2,1)S(1)} %slice_select_fusion), channel_id=1, replica_groups=mesh['frame'=8,'pos'=16] {'frame'}, dimensions={0}, use_global_device_ids=true | all-gather | bytes 294912 | tf_op jit(solution)/shard_map/all_gather | solution.py:11
  36.6 1.4 pad_maximum_fusion
  38.0 26.5 %all_to_all.15 = bf16[16,3,64,256]{3,2,1,0:T(8,128)(2,1)S(1)} all-to-all(bf16[16,3,64,256]{3,2,1,0:T(8,128)(2,1)S(1)} %pad_maximum_fusion), channel_id=1, replica_groups=mesh['frame'=8,'pos'=16] {'pos'}, dimensions={0} | all-to-all | bytes 3145728 | tf_op jit(solution)/shard_map/all_to_all | solution.py:71
  64.5 0.3 multiply_reduce_fusion.3
  65.0 0.2 multiply_reduce_fusion.4
  65.2 0.5 copy-done.1
  65.7 1.5 copy_convert_fusion
  67.2 0.3 fusion.18
  67.6 1.4 convolution_convert_fusion.3
  69.0 1.2 slice_convert_fusion
  70.2 0.2 fusion.35
  70.4 1.1 convolution_convert_fusion.6
  71.5 1.4 convolution_convert_fusion.5
  72.9 1.1 convolution_convert_fusion.7
  74.1 4.5 %reshape.132 = bf16[2,1024,4,64]{3,2,1,0:T(4,128)(2,1)} reshape(bf16[2048,256]{1,0:T(8,128)(2,1)} %convolution_convert_fusion.3) | data formatting | bytes 2097152 | tf_op jit(solution)/shard_map/reshape;reshape | solution.py:31
  78.5 4.1 %copy.61 = bf16[2,1024,4,64]{1,3,2,0:T(8,128)(2,1)} copy(bf16[2,1024,4,64]{3,2,1,0:T(4,128)(2,1)} %reshape.132) | data formatting | bytes 2097152 | tf_op jit(solution)/shard_map/reshape;reshape | solution.py:31
  82.6 1.4 convolution_convert_fusion.4
  84.0 4.5 %reshape.131 = bf16[2,1024,4,64]{3,2,1,0:T(4,128)(2,1)} reshape(bf16[2048,256]{1,0:T(8,128)(2,1)} %convolution_convert_fusion.4) | data formatting | bytes 2097152 | tf_op jit(solution)/shard_map/reshape;reshape | solution.py:31
  88.6 1.9 reshape.130
  90.4 4.2 %copy.58 = bf16[2,1024,4,64]{1,3,2,0:T(8,128)(2,1)} copy(bf16[2,1024,4,64]{3,2,1,0:T(4,128)(2,1)} %reshape.130) | data formatting | bytes 2097152 | tf_op jit(solution)/shard_map/reshape;reshape | solution.py:31
  94.6 1.2 broadcast_in_dim.19
  95.8 24.7 %multiply_reduce_fusion = (f32[2,4,1024]{2,1,0:T(4,128)S(1)}, f32[2,4,1024,2048]{3,2,1,0:T(8,128)}) fusion(bf16[2,1024,4,64]{1,3,2,0:T(8,128)(2,1)S(1)} %broadcast_in_dim.19, bf16[2,1024,4,64]{1,3,2,0:T(8,128)(2,1)S(1)} %copy-done.3, bf16[2,1024,4,64]{3,2,1,0:T(4,128)(2,1)} %reshape.131), kind=kOutput, calls=%fused_computation.1 | convolution fusion | flops 2185224192 | bytes 70287360 | tf_op jit(solution)/shard_map/fphd,fkhd->fhpk/dot_general | solution.py:36
  120.5 21.2 %fusion = f32[2,4,1024]{2,1,0:T(4,128)S(1)} fusion(f32[2,4,1024,2048]{3,2,1,0:T(8,128)} %get-tuple-element.6, f32[2,4,1024]{2,1,0:T(4,128)S(1)} %get-tuple-element.5), kind=kLoop, calls=%fused_computation.2 | loop fusion | flops 50323456 | bytes 67174400 | tf_op jit(solution)/shard_map/reduce_sum | solution.py:38
  141.8 2.2 broadcast_in_dim.17
  144.0 24.9 %fusion.24 = bf16[2,1024,4,64]{1,3,2,0:T(8,128)(2,1)} fusion(f32[2,4,1024,2048]{3,2,1,0:T(8,128)} %get-tuple-element.6, f32[2,4,1024]{2,1,0:T(4,128)S(1)} %get-tuple-element.5, bf16[2,1024,4,64]{1,3,2,0:T(8,128)(2,1)} %broadcast_in_dim.17, bf16[2,1024,4,64]{1,3,2,0:T(8,128)(2,1)S(1)} %copy-done.4, f32[2,1024,4]{1,2,0:T(4,128)S(1)} %bitcast.86), kind=kOutput, calls=%fused_computation.38 | convolution fusion | flops 2203058176 | bytes 70320128 | tf_op jit(solution)/shard_map/fhpk,fkhd->fphd/dot_general | solution.py:39
  168.9 1.7 fusion.19
  170.7 0.1 copy.64
  170.8 27.2 %all_to_all.16 = bf16[128,2,8,256]{3,2,1,0:T(8,128)(2,1)S(1)} all-to-all(bf16[128,2,8,256]{3,2,1,0:T(8,128)(2,1)S(1)} %bitcast.78), channel_id=1, replica_groups=mesh['frame'=8,'pos'=16] {'frame','pos'}, dimensions={0} | all-to-all | bytes 2097152 | tf_op jit(solution)/shard_map/all_to_all | solution.py:99
  197.9 0.5 multiply_reduce_fusion.2
  198.4 0.1 add_rsqrt_fusion
  198.5 0.2 rsqrt.38
  198.7 0.3 fusion.22
  199.1 0.4 convolution_convert_fusion.1
  199.5 1.8 reshape_reshape.22
  201.3 0.4 convolution_convert_fusion
  201.8 1.9 reshape_reshape.23
  203.7 1.4 convolution_convert_fusion.2
  205.1 4.6 %reshape_reshape.21 = bf16[256,8,4,64]{3,2,1,0:T(4,128)(2,1)} reshape(bf16[2048,256]{1,0:T(8,128)(2,1)} %convolution_convert_fusion.2) | data formatting | bytes 2097152 | tf_op jit(solution)/shard_map/reshape;reshape | solution.py:31
  209.7 3.6 %multiply_reduce_fusion.1 = (f32[8,4,256]{2,1,0:T(4,128)S(1)}, f32[8,4,256,256]{2,3,1,0:T(8,128)S(1)}) fusion(bf16[256,8,4,64]{3,2,1,0:T(4,128)(2,1)} %reshape_reshape.23, bf16[256,8,4,64]{3,2,1,0:T(4,128)(2,1)S(1)} %copy-done.2), kind=kOutput, calls=%fused_computation.6 | convolution fusion | flops 272621568 | bytes 10518528 | tf_op jit(solution)/shard_map/fphd,kphd->phfk/dot_general | solution.py:36
  213.2 1.5 fusion.4
  214.8 1.9 fusion.20
  216.8 0.2 bitcast_convert_fusion
  217.0 0.7 copy-done.13
  217.7 0.9 fusion.23
  218.6 0.1 copy.71
  218.7 19.6 %all_to_all.17 = bf16[8,32,8,256]{3,1,2,0:T(8,128)(2,1)S(1)} all-to-all(bf16[8,32,8,256]{3,1,2,0:T(8,128)(2,1)S(1)} %copy.71), channel_id=1, replica_groups=mesh['frame'=8,'pos'=16] {'frame'}, dimensions={0} | all-to-all | bytes 2097152 | tf_op jit(solution)/shard_map/all_to_all | solution.py:115
  238.2 1.6 copy.72
  (36 shorter events, 0.4 us)
Async XLA Ops:
  0.0 67.6 %copy-start = (bf16[256,256]{1,0:T(8,128)(2,1)S(1)}, bf16[256,256]{1,0:T(8,128)(2,1)}, u32[]{:S(2)}) copy-start(bf16[256,256]{1,0:T(8,128)(2,1)} %param.14) | copy-start | bytes 393220
  64.5 1.2 copy-start.1
  64.9 2.3 copy-start.14
  69.0 2.5 %copy-start.7 = (bf16[256,256]{1,0:T(8,128)(2,1)S(1)}, bf16[256,256]{1,0:T(8,128)(2,1)}, u32[]{:S(2)}) copy-start(bf16[256,256]{1,0:T(8,128)(2,1)} %param.15) | copy-start | bytes 393220
  78.5 4.1 %copy-start.8 = (bf16[256,256]{1,0:T(8,128)(2,1)S(1)}, bf16[256,256]{1,0:T(8,128)(2,1)}, u32[]{:S(2)}) copy-start(bf16[256,256]{1,0:T(8,128)(2,1)} %param.13) | copy-start | bytes 393220
  84.0 4.5 %copy-start.5 = (bf16[2048,256]{1,0:T(8,128)(2,1)S(1)}, bf16[2048,256]{1,0:T(8,128)(2,1)}, u32[]{:S(2)}) copy-start(bf16[2048,256]{1,0:T(8,128)(2,1)} %convolution_convert_fusion.5) | copy-start | bytes 3145732
  90.4 5.3 %copy-start.3 = (bf16[2,1024,4,64]{1,3,2,0:T(8,128)(2,1)S(1)}, bf16[2,1024,4,64]{1,3,2,0:T(8,128)(2,1)}, u32[]{:S(2)}) copy-start(bf16[2,1024,4,64]{1,3,2,0:T(8,128)(2,1)} %copy.61) | copy-start | bytes 3145732
  141.8 2.2 copy-start.4
  144.0 24.9 %copy-start.9 = (bf16[256,256]{1,0:T(8,128)(2,1)S(1)}, bf16[256,256]{1,0:T(8,128)(2,1)}, u32[]{:S(2)}) copy-start(bf16[256,256]{1,0:T(8,128)(2,1)} %param.16) | copy-start | bytes 393220
  170.8 28.0 %copy-start.15 = (f32[256]{0:T(256)S(1)}, f32[256]{0:T(256)}, u32[]{:S(2)}) copy-start(f32[256]{0:T(256)} %param.17) | copy-start | bytes 3076
  197.9 1.1 copy-start.10
  199.5 1.8 copy-start.11
  201.8 1.9 copy-start.12
  205.1 4.6 %copy-start.2 = (bf16[256,8,4,64]{3,2,1,0:T(4,128)(2,1)S(1)}, bf16[256,8,4,64]{3,2,1,0:T(4,128)(2,1)}, u32[]{:S(2)}) copy-start(bf16[256,8,4,64]{3,2,1,0:T(4,128)(2,1)} %reshape_reshape.22) | copy-start | bytes 3145732
  213.2 1.6 copy-start.6
  216.8 0.9 copy-start.13
